TPU v7x, 32 devices: a whole 2x2x4 slice. The times are simulated.
32 devices in a mesh: dp: 8 (over y, x, core), tensor: 4 (over z).
Axes of the slice: x: 2, y: 2, z: 4, core: 2. Of those that a mesh axis runs over, the one named last changes fastest.
Arguments:
- tokens: bfloat16 [8192, 2048], P(('dp', 'tensor')), may hold values from -6 to 6
- seq_start: int32 [8192], P('dp'), may hold values from 0 to 8191, as said below
- proj_weight: bfloat16 [2048, 3, 2048], P('dp', None, 'tensor'), may hold values from -0.125 to 0.125
- proj_bias: bfloat16 [3, 8, 256], P(None, 'tensor', 'dp'), may hold values from -3 to 3
- out_weight: bfloat16 [2048, 2048], P('tensor', 'dp'), may hold values from -1.5 to 1.5
- up_weight: bfloat16 [2048, 8192], P('dp', 'tensor'), may hold values from -0.125 to 0.125
- up_bias: bfloat16 [4, 2048], P('tensor', 'dp'), may hold values from -3 to 3
- down_weight: bfloat16 [8192, 2048], P('tensor', 'dp'), may hold values from -0.0625 to 0.0625
- norm_gains: bfloat16 [2, 2048], P(None, ('dp', 'tensor')), may hold values from 0.099609375 to 1.8984375
- biases: bfloat16 [4, 2048], P(None, ('dp', 'tensor')), may hold values from -3 to 3
- cotangent: bfloat16 [8192, 2048], P(('dp', 'tensor')), may hold values from -6 to 6
Outputs:
- output: bfloat16 [8192, 2048], P(('dp', 'tensor'))
- input_grad: float32 [8192, 2048], P(('dp', 'tensor'))
- proj_grad: float32 [2048, 3, 2048], P('dp', None, 'tensor')
- proj_bias_grad: float32 [3, 8, 256], P(None, 'tensor', 'dp')
- out_grad: float32 [2048, 2048], P('tensor', 'dp')
- up_grad: float32 [2048, 8192], P('dp', 'tensor')
- up_bias_grad: float32 [4, 2048], P('tensor', 'dp')
- down_grad: float32 [8192, 2048], P('tensor', 'dp')
- gains_grad: float32 [2, 2048], P(None, ('dp', 'tensor'))
- biases_grad: float32 [4, 2048], P(None, ('dp', 'tensor'))
Inputs may be any that keep to these rules, and one draw needn't show every extreme that they name: seq_start never falls along the tokens, is at most the token's own index, and every sequence lies inside one aligned block of 1024 tokens (the tokens of one index of dp); some block other than the last holds a single sequence of 1024 tokens, the others hold sequences of uneven lengths, and the last token begins a sequence of its own.
All inputs are finite; a program needn't handle non-finite values.
Results may differ from a plain program's by a relative error of at most 0.012.
Values may be sent and summed in bfloat16 or wider, within the bound.
No kernel may reach another device: no remote copies, remote signals or barrier semaphores. Data moves between devices by JAX's collectives and lax.ppermute only.
A program may use at most 192 MiB of HBM per device.

v0:
```python
import jax
import jax.numpy as jnp
from jax import lax
from jax.sharding import PartitionSpec as P

ROT = 64
EPSILON = 1e-05
ROTARY_BASE = 10000.0


def layer_norm(values, gain_row, shift_row):
    centered = values - jnp.mean(values, axis=-1, keepdims=True)
    spread = jnp.mean(centered * centered, axis=-1, keepdims=True)
    return centered * lax.rsqrt(spread + EPSILON) * gain_row + shift_row


def both_norms(values, gain_rows, shift_rows):
    return (
        layer_norm(values, gain_rows[0], shift_rows[0]),
        layer_norm(values, gain_rows[1], shift_rows[1]),
    )


def gelu_exact(inputs):
    return jax.nn.gelu(inputs, approximate=False)


def rotate(values, positions, turn_sign):
    half_rot = ROT // 2
    frequency = ROTARY_BASE ** (-(jnp.arange(half_rot, dtype=jnp.float32) * 2.0) / ROT)
    angles = positions.astype(jnp.float32)[:, None] * frequency[None, :]
    cosine = jnp.cos(angles)[:, None, :]
    sine_term = turn_sign * jnp.sin(angles)[:, None, :]
    first_half = values[..., :half_rot]
    second_half = values[..., half_rot:ROT]
    return jnp.concatenate(
        [
            first_half * cosine - second_half * sine_term,
            second_half * cosine + first_half * sine_term,
            values[..., ROT:],
        ],
        axis=-1,
    )


def masked_scores(query_block, key_rows, starts, block_start, block_rows):
    row_count = key_rows.shape[0]
    score_scale = key_rows.shape[-1] ** (-0.5)
    key_index = jnp.arange(row_count, dtype=jnp.int32)
    query_begin = lax.dynamic_slice_in_dim(starts, block_start, block_rows, 0)
    query_index = block_start + jnp.arange(block_rows, dtype=jnp.int32)
    scores = (
        jnp.einsum("qhe,khe->hqk", query_block, key_rows, preferred_element_type=jnp.float32)
        * score_scale
    )
    allowed = (query_begin[:, None] == starts[None, :]) & (
        key_index[None, :] <= query_index[:, None]
    )
    return jnp.where(allowed[None], scores, -1e30)


def attention_forward(queries, key_rows, value_rows, starts, block_rows):
    row_count = queries.shape[0]

    def one_block(block_start):
        query_block = lax.dynamic_slice_in_dim(queries, block_start, block_rows, 0)
        scores = masked_scores(query_block, key_rows, starts, block_start, block_rows)
        row_max = jnp.max(scores, axis=-1, keepdims=True)
        powers = jnp.exp(scores - row_max)
        row_total = jnp.sum(powers, axis=-1, keepdims=True)
        weights = (powers / row_total).astype(jnp.bfloat16)
        attended = jnp.einsum(
            "hqk,khe->qhe", weights, value_rows, preferred_element_type=jnp.float32
        )
        return (attended, (row_max + jnp.log(row_total))[..., 0])

    block_starts = jnp.arange(row_count // block_rows, dtype=jnp.int32) * block_rows
    attended, log_total = lax.map(one_block, block_starts)
    return (attended.reshape(queries.shape), log_total)


def attention_backward(queries, key_rows, value_rows, starts, log_total, grad_attended, block_rows):
    row_count = queries.shape[0]
    score_scale = queries.shape[-1] ** (-0.5)

    def one_block(accumulated, pieces):
        block_start, block_total = pieces
        grad_keys, grad_values = accumulated
        query_block = lax.dynamic_slice_in_dim(queries, block_start, block_rows, 0)
        grad_block = lax.dynamic_slice_in_dim(grad_attended, block_start, block_rows, 0)
        scores = masked_scores(query_block, key_rows, starts, block_start, block_rows)
        probs = jnp.exp(scores - block_total[..., None])
        grad_values = grad_values + jnp.einsum(
            "hqk,qhe->khe",
            probs.astype(jnp.bfloat16),
            grad_block,
            preferred_element_type=jnp.float32,
        )
        grad_probs = jnp.einsum(
            "qhe,khe->hqk", grad_block, value_rows, preferred_element_type=jnp.float32
        )
        inner_sum = jnp.sum(probs * grad_probs, axis=-1, keepdims=True)
        grad_scores = (probs * (grad_probs - inner_sum)).astype(jnp.bfloat16)
        grad_query = (
            jnp.einsum("hqk,khe->qhe", grad_scores, key_rows, preferred_element_type=jnp.float32)
            * score_scale
        )
        grad_keys = (
            grad_keys
            + jnp.einsum(
                "hqk,qhe->khe", grad_scores, query_block, preferred_element_type=jnp.float32
            )
            * score_scale
        )
        return ((grad_keys, grad_values), grad_query)

    block_starts = jnp.arange(row_count // block_rows, dtype=jnp.int32) * block_rows
    zeros_like_keys = jnp.zeros(queries.shape, jnp.float32)
    (grad_keys, grad_values), grad_queries = lax.scan(
        one_block, (zeros_like_keys, zeros_like_keys), (block_starts, log_total)
    )
    return (grad_queries.reshape(queries.shape), grad_keys, grad_values)


def shards(
    tokens,
    seq_start,
    proj_weight,
    proj_bias,
    out_weight,
    up_weight,
    up_bias,
    down_weight,
    norm_gains,
    biases,
    cotangent,
):
    local_rows = tokens.shape[0]
    row_count = local_rows * lax.axis_size("tensor")
    block_rows = min(512, row_count)
    dp_index = lax.axis_index("dp")
    gathered = (
        lax.all_gather(proj_weight, "dp", axis=0, tiled=True),
        lax.all_gather(proj_bias, "dp", axis=2, tiled=True),
        lax.all_gather(out_weight, "dp", axis=1, tiled=True),
        lax.all_gather(up_weight, "dp", axis=0, tiled=True),
        lax.all_gather(up_bias, "dp", axis=1, tiled=True),
        lax.all_gather(down_weight, "dp", axis=1, tiled=True),
    )
    joined_weight, joined_bias, mix_weight, hidden_weight, hidden_bias, back_weight = gathered
    gain_rows, shift_rows = (
        lax.all_gather(norm_gains, ("dp", "tensor"), axis=1, tiled=True),
        lax.all_gather(biases, ("dp", "tensor"), axis=1, tiled=True),
    )
    gain_rows = gain_rows.astype(jnp.float32)
    shift_rows = shift_rows.astype(jnp.float32)
    local_f = tokens.astype(jnp.float32)
    first_local, second_local = both_norms(local_f, gain_rows, shift_rows)
    first_rows, second_rows = (
        lax.all_gather(first_local.astype(jnp.bfloat16), "tensor", axis=0, tiled=True),
        lax.all_gather(second_local.astype(jnp.bfloat16), "tensor", axis=0, tiled=True),
    )
    heads_here = joined_bias.shape[1]
    head_size = joined_bias.shape[2]
    local_width = heads_here * head_size
    projected = jnp.einsum(
        "nd,dch->nch", first_rows, joined_weight, preferred_element_type=jnp.float32
    ) + joined_bias.astype(jnp.float32).reshape(3, local_width)
    positions = dp_index * row_count + jnp.arange(row_count, dtype=jnp.int32) - seq_start
    queries = rotate(
        projected[:, 0].reshape(row_count, heads_here, head_size), positions, 1.0
    ).astype(jnp.bfloat16)
    key_rows = rotate(
        projected[:, 1].reshape(row_count, heads_here, head_size), positions, 1.0
    ).astype(jnp.bfloat16)
    value_rows = projected[:, 2].reshape(row_count, heads_here, head_size).astype(jnp.bfloat16)
    attended, log_total = attention_forward(queries, key_rows, value_rows, seq_start, block_rows)
    attended = attended.reshape(row_count, local_width).astype(jnp.bfloat16)
    hidden = jnp.dot(
        second_rows, hidden_weight, preferred_element_type=jnp.float32
    ) + hidden_bias.astype(jnp.float32)
    activated = gelu_exact(hidden).astype(jnp.bfloat16)
    attn_part = jnp.dot(attended, mix_weight, preferred_element_type=jnp.float32)
    branches = lax.psum_scatter(
        attn_part + jnp.dot(activated, back_weight, preferred_element_type=jnp.float32),
        "tensor",
        scatter_dimension=0,
        tiled=True,
    )
    output = (local_f + branches + shift_rows[2] + shift_rows[3]).astype(jnp.bfloat16)
    grad_rows = lax.all_gather(cotangent, "tensor", axis=0, tiled=True)
    regathered = (
        lax.all_gather(proj_weight, "dp", axis=0, tiled=True),
        lax.all_gather(proj_bias, "dp", axis=2, tiled=True),
        lax.all_gather(out_weight, "dp", axis=1, tiled=True),
        lax.all_gather(up_weight, "dp", axis=0, tiled=True),
        lax.all_gather(up_bias, "dp", axis=1, tiled=True),
        lax.all_gather(down_weight, "dp", axis=1, tiled=True),
    )
    joined_again, _, mix_again, hidden_again, _, back_again = regathered
    grad_active = jnp.einsum("nd,fd->nf", grad_rows, back_again, preferred_element_type=jnp.float32)
    down_term = jnp.einsum("nf,nd->fd", activated, grad_rows, preferred_element_type=jnp.float32)
    _, gelu_back = jax.vjp(gelu_exact, hidden)
    grad_hidden = gelu_back(grad_active)[0].astype(jnp.bfloat16)
    up_term = jnp.einsum("nd,nf->df", second_rows, grad_hidden, preferred_element_type=jnp.float32)
    up_bias_term = jnp.sum(grad_hidden, axis=0, keepdims=True, dtype=jnp.float32)
    grad_second = jnp.einsum(
        "nf,df->nd", grad_hidden, hidden_again, preferred_element_type=jnp.float32
    )
    grad_attended = jnp.einsum(
        "nd,ed->ne", grad_rows, mix_again, preferred_element_type=jnp.float32
    ).astype(jnp.bfloat16)
    mix_term = jnp.einsum("ne,nd->ed", attended, grad_rows, preferred_element_type=jnp.float32)
    query_back, key_back, value_back = attention_backward(
        queries,
        key_rows,
        value_rows,
        seq_start,
        log_total,
        grad_attended.reshape(row_count, heads_here, head_size),
        block_rows,
    )
    query_back = rotate(query_back, positions, -1.0).reshape(row_count, local_width)
    key_back = rotate(key_back, positions, -1.0).reshape(row_count, local_width)
    grad_projected = jnp.stack(
        [query_back, key_back, value_back.reshape(row_count, local_width)], axis=1
    ).astype(jnp.bfloat16)
    joined_term = jnp.einsum(
        "nd,nch->dch", first_rows, grad_projected, preferred_element_type=jnp.float32
    )
    joined_bias_term = jnp.sum(grad_projected, axis=0, dtype=jnp.float32).reshape(
        3, heads_here, head_size
    )
    grad_first = jnp.einsum(
        "nch,dch->nd", grad_projected, joined_again, preferred_element_type=jnp.float32
    )
    grad_local = cotangent.astype(jnp.float32)
    first_sum, second_sum = (
        lax.psum_scatter(
            grad_first.astype(jnp.bfloat16), "tensor", scatter_dimension=0, tiled=True
        ).astype(jnp.float32),
        lax.psum_scatter(
            grad_second.astype(jnp.bfloat16), "tensor", scatter_dimension=0, tiled=True
        ).astype(jnp.float32),
    )
    _, norm_back = jax.vjp(both_norms, local_f, gain_rows, shift_rows)
    grad_norm_in, gain_term, shift_term = norm_back((first_sum, second_sum))
    input_grad = grad_local + grad_norm_in
    column_sums = jnp.sum(grad_local, axis=0)
    shift_term = jnp.concatenate([shift_term[:2], jnp.stack([column_sums, column_sums])], axis=0)
    gains_grad, biases_grad = (
        lax.psum_scatter(gain_term, ("dp", "tensor"), scatter_dimension=1, tiled=True),
        lax.psum_scatter(shift_term, ("dp", "tensor"), scatter_dimension=1, tiled=True),
    )
    summed = (
        lax.psum_scatter(joined_term, "dp", scatter_dimension=0, tiled=True),
        lax.psum_scatter(joined_bias_term, "dp", scatter_dimension=2, tiled=True),
        lax.psum_scatter(mix_term, "dp", scatter_dimension=1, tiled=True),
        lax.psum_scatter(up_term, "dp", scatter_dimension=0, tiled=True),
        lax.psum_scatter(up_bias_term, "dp", scatter_dimension=1, tiled=True),
        lax.psum_scatter(down_term, "dp", scatter_dimension=1, tiled=True),
    )
    return (
        output,
        input_grad,
        summed[0],
        summed[1],
        summed[2],
        summed[3],
        summed[4],
        summed[5],
        gains_grad,
        biases_grad,
    )


def solution(mesh):
    in_specs = (
        P(("dp", "tensor"), None),
        P("dp"),
        P("dp", None, "tensor"),
        P(None, "tensor", "dp"),
        P("tensor", "dp"),
        P("dp", "tensor"),
        P("tensor", "dp"),
        P("tensor", "dp"),
        P(None, ("dp", "tensor")),
        P(None, ("dp", "tensor")),
        P(("dp", "tensor"), None),
    )
    out_specs = (
        P(("dp", "tensor"), None),
        P(("dp", "tensor"), None),
        P("dp", None, "tensor"),
        P(None, "tensor", "dp"),
        P("tensor", "dp"),
        P("dp", "tensor"),
        P("tensor", "dp"),
        P("tensor", "dp"),
        P(None, ("dp", "tensor")),
        P(None, ("dp", "tensor")),
    )
    return jax.shard_map(shards, mesh=mesh, in_specs=in_specs, out_specs=out_specs, check_vma=False)
```

profile of v0, /device:TPU:0, one launch (start us, length us, event | category | flops | bytes accessed | tf_op | source)
XLA Modules:
  0.0 1526.1 jit_solution(3073304048536600505)
XLA Ops:
  8.7 71.2 %all-gather = bf16[32,64,2]{1,2,0:T(2,128)(2,1)S(1)} all-gather(bf16[1,64,2]{1,2,0:T(2,128)(2,1)} %bitcast.182), channel_id=1, replica_groups=mesh['dp'=8,'tensor'=4] {'dp','tensor'}, dimensions={0}, use_global_device_ids=true | all-gather | bytes 8448 | tf_op jit(solution)/shard_map/all_gather | solution.py:152
  80.0 66.0 %all-gather.1 = bf16[32,64,4]{1,2,0:T(4,128)(2,1)S(1)} all-gather(bf16[1,64,4]{1,2,0:T(4,128)(2,1)} %bitcast.181), channel_id=1, replica_groups=mesh['dp'=8,'tensor'=4] {'dp','tensor'}, dimensions={0}, use_global_device_ids=true | all-gather | bytes 16896 | tf_op jit(solution)/shard_map/all_gather | solution.py:153
  155.9 8.2 all_gather.45
  164.7 9.5 all_gather.41
  174.4 3.2 broadcast_multiply_fusion
  177.6 6.2 convolution_convert_fusion.1
  183.8 47.5 %all-gather.10.cloned.1.call-done = bf16[1024,2048]{1,0:T(8,128)(2,1)} async-done(((bf16[256,2048]{1,0:T(8,128)(2,1)}), bf16[1024,2048]{1,0:T(8,128)(2,1)}) %all-gather.10.cloned.1.call-update) | async-done | bytes 4194320 | tf_op jit(solution)/shard_map/all_gather | solution.py:160
  231.3 47.4 %all-gather.12.cloned.1.call-done = bf16[2048,3,512]{0,2,1:T(8,128)(2,1)} async-done(((bf16[256,3,512]{0,2,1:T(8,128)(2,1)}), bf16[2048,3,512]{0,2,1:T(8,128)(2,1)}) %all-gather.12.cloned.1.call-update) | async-done | bytes 6291472 | tf_op jit(solution)/shard_map/all_gather | solution.py:143
  278.7 10.1 broadcast_add_fusion
  293.2 4.0 fusion.73
  299.6 2.2 copy.178
  301.8 2.5 slice.104
  308.2 2.3 copy.180
  312.4 2.3 copy.177
  316.0 2.3 copy.176
  318.3 3.2 subtract_convert_fusion.2
  321.5 3.2 pad_maximum_fusion.1
  324.7 20.5 %while.27 = (s32[]{:T(128)}, bf16[2,512,2,256]{3,1,2,0:T(8,128)(2,1)}, f32[2,2,512]{2,1,0:T(2,128)S(1)}, s32[2]{0:T(128)S(1)}, s32[1024]{0:T(1024)S(1)}, /*index...) while((s32[]{:T(128)}, ...), condition=%wide.region_5.6_spmd, body=%wide.region_2.5_spmd.sunk | while | flops 1087897088 | bytes 26786032 | solution.py:78
  328.8 2.7 fusion.131
  338.9 2.7 fusion.131
  345.2 30.7 %while.28 = (s32[]{:T(128)}, f32[1024,2,256]{0,2,1:T(8,128)S(1)}, f32[1024,2,256]{0,2,1:T(8,128)}, f32[2,512,2,256]{3,1,0,2:T(8,128)}, s32[2]{0:T(128)S(1)}, /*i...) while((s32[]{:T(128)}, f32[1024,2,256]{0,2,1:T(8,128)S(1)}, ...), condition=%wide.region_12.13_spmd.clone, body=%wide.region_10.12_spmd.clone.sunk | while | flops 2704539136 | bytes 94415280 | solution.py:119
  380.9 3.9 subtract_convert_fusion.1
  389.7 3.2 convert.66
  394.5 11.4 bitcast_convert_fusion
  406.0 10.0 all-gather.18.cloned.1.call-done
  416.0 14.8 fusion.78
  430.8 42.9 %all-gather.20.cloned.1.call-done = bf16[2048,2048]{1,0:T(8,128)(2,1)} async-done(((bf16[2048,256]{1,0:T(8,128)(2,1)}), bf16[2048,2048]{1,0:T(8,128)(2,1)}) %all-gather.20.cloned.1.call-update) | async-done | bytes 8388624 | tf_op jit(solution)/shard_map/all_gather | solution.py:148
  473.8 33.0 %convert_reduce_fusion = (f32[2048]{0:T(1024)S(1)}, bf16[1024,2048]{1,0:T(8,128)(2,1)S(1)}, f32[1024,2048]{1,0:T(8,128)}) fusion(f32[1024,2048]{1,0:T(8,128)} %fusion.78, f32[2048]{0:T(1024)S(1)} %bitcast.166, bf16[1024,2048]{1,0:T(8,128)(2,1)} %all-gather.22.cloned.1.call-done, bf16[2048,2048]{1,0:T(8,128)(2,1)} %all-gather.20.cloned.1.call-done), kind=kOutput, calls=%fused_computation.50 | convolution fusion | flops 8747218944 | bytes 33570816 | tf_op jit(solution)/shard_map/nd,fd->nf/dot_general | solution.py:201
  508.7 10.9 convolution_convert_fusion
  522.2 10.0 multiply_convert_fusion.1
  532.2 12.7 fusion.79
  545.0 5.6 convolution_add_fusion
  556.6 75.9 %reduce-scatter.22.cloned.1.call-done = bf16[256,2048]{1,0:T(8,128)(2,1)} async-done(((bf16[1024,2048]{1,0:T(8,128)(2,1)}), bf16[256,2048]{1,0:T(8,128)(2,1)}) %reduce-scatter.22.cloned.1.call-update) | async-done | bytes 1048592 | tf_op jit(solution)/shard_map/reduce_scatter | solution.py:242
  632.5 2.7 fusion.62
  635.3 3.3 fusion.67
  640.1 139.7 %reduce-scatter.20.cloned.1.call-done = f32[256,2048]{1,0:T(8,128)} async-done(((f32[1024,2048]{1,0:T(8,128)}), f32[256,2048]{1,0:T(8,128)}) %reduce-scatter.20.cloned.1.call-update) | async-done | bytes 2097168 | tf_op jit(solution)/shard_map/reduce_scatter | solution.py:184
  779.9 5.0 convert_reduce_fusion.5
  786.6 6.5 fusion.80
  795.0 11.6 fusion.41
  806.7 15.3 %fusion.82 = f32[2048,2048]{1,0:T(8,128)} fusion(bf16[1024,2048]{1,0:T(8,128)(2,1)} %multiply_convert_fusion.1, bf16[1024,2048]{1,0:T(8,128)(2,1)} %all-gather.22.cloned.1.call-done), kind=kOutput, calls=%fused_computation.157 | convolution fusion | flops 8589934592 | bytes 25165824 | tf_op jit(solution)/shard_map/nf,nd->fd/dot_general | solution.py:202
  822.4 15.3 %fusion.81 = f32[2048,2048]{1,0:T(8,128)} fusion(bf16[1024,2048]{1,0:T(8,128)(2,1)} %all-gather.16.cloned.1.call-done, bf16[1024,2048]{1,0:T(8,128)(2,1)} %copy-done.45), kind=kOutput, calls=%fused_computation.156 | convolution fusion | flops 8589934592 | bytes 25165824 | tf_op jit(solution)/shard_map/nd,nf->df/dot_general | solution.py:205
  839.3 16.8 %reduce-scatter.36.cloned.1.call-done = f32[256,1]{1,0:T(8,128)} async-done(((f32[2048,1]{1,0:T(8,128)}), f32[256,1]{1,0:T(8,128)}) %reduce-scatter.36.cloned.1.call-update) | async-done | bytes 1040
  857.6 138.1 %reduce-scatter.38.cloned.1.call-done = f32[64,2]{1,0:T(8,128)} async-done(((f32[2048,2]{1,0:T(8,128)}), f32[64,2]{1,0:T(8,128)}) %reduce-scatter.38.cloned.1.call-update) | async-done | bytes 528
  997.1 134.3 %reduce-scatter.40.cloned.1.call-done = f32[64,4]{1,0:T(8,128)} async-done(((f32[2048,4]{1,0:T(8,128)}), f32[64,4]{1,0:T(8,128)}) %reduce-scatter.40.cloned.1.call-update) | async-done | bytes 1040
  1132.9 49.8 %reduce-scatter.28.cloned.1.call-done = f32[512,256]{1,0:T(8,128)} async-done(((f32[512,2048]{1,0:T(8,128)}), f32[512,256]{1,0:T(8,128)}) %reduce-scatter.28.cloned.1.call-update) | async-done | bytes 524304 | tf_op jit(solution)/shard_map/reduce_scatter | solution.py:258
  1182.7 96.0 %reduce-scatter.26.cloned.1.call-done = f32[256,3,512]{2,0,1:T(8,128)} async-done(((f32[2048,3,512]{2,0,1:T(8,128)}), f32[256,3,512]{2,0,1:T(8,128)}) %reduce-scatter.26.cloned.1.call-update) | async-done | bytes 1572880 | tf_op jit(solution)/shard_map/reduce_scatter | solution.py:256
  1278.8 120.0 %reduce-scatter.32.cloned.1.call-done = f32[2048,256]{1,0:T(8,128)} async-done(((f32[2048,2048]{1,0:T(8,128)}), f32[2048,256]{1,0:T(8,128)}) %reduce-scatter.32.cloned.1.call-update) | async-done | bytes 2097168 | tf_op jit(solution)/shard_map/reduce_scatter | solution.py:261
  1398.8 120.2 %reduce-scatter.30.cloned.1.call-done = f32[256,2048]{1,0:T(8,128)} async-done(((f32[2048,2048]{1,0:T(8,128)}), f32[256,2048]{1,0:T(8,128)}) %reduce-scatter.30.cloned.1.call-update) | async-done | bytes 2097168 | tf_op jit(solution)/shard_map/reduce_scatter | solution.py:259
  (251 shorter events, 96.7 us)
Async XLA Ops:
  7.2 143.3 %copy-start.1 = (bf16[256,2048]{1,0:T(8,128)(2,1)S(1)}, bf16[256,2048]{1,0:T(8,128)(2,1)}, u32[]{:S(2)}) copy-start(bf16[256,2048]{1,0:T(8,128)(2,1)} %param.15) | copy-start | bytes 3145732
  7.2 145.4 %copy-start.28 = (bf16[256,3,512]{2,0,1:T(8,128)(2,1)S(1)}, bf16[256,3,512]{2,0,1:T(8,128)(2,1)}, u32[]{:S(2)}) copy-start(bf16[256,3,512]{2,0,1:T(8,128)(2,1)} %param.17) | copy-start | bytes 2359300
  7.2 170.4 %all-gather.14.cloned.1.call-start = ((), (), s32[]{:S(2)}) async-start(), calls=%async_computation.13 | async-start | bytes 2359296 | tf_op jit(solution)/shard_map/all_gather | solution.py:145
  7.9 169.6 %all-gather.22.cloned.1.call-start = ((), (), s32[]{:S(2)}) async-start(), calls=%async_computation.18 | async-start | bytes 5242880 | tf_op jit(solution)/shard_map/all_gather | solution.py:191
  8.7 222.6 %all-gather.10.cloned.1.call-start = ((), (), s32[]{:S(2)}) async-start(), calls=%async_computation.11 | async-start | bytes 5242880 | tf_op jit(solution)/shard_map/all_gather | solution.py:160
  147.6 6.8 copy-start.33
  149.3 5.7 copy-start.38
  150.5 5.4 copy-start.43
  150.5 14.2 copy-start.42
  152.5 21.9 %copy-start.24 = (s32[1024]{0:T(1024)S(1)}, s32[1024]{0:T(1024)}, u32[]{:S(2)}) copy-start(s32[1024]{0:T(1024)} %param.16) | copy-start | bytes 12292
  152.5 126.2 %all-gather.12.cloned.1.call-start = ((), (), s32[]{:S(2)}) async-start(), calls=%async_computation.12 | async-start | bytes 7077888 | tf_op jit(solution)/shard_map/all_gather | solution.py:143
  153.8 252.2 %all-gather.16.cloned.1.call-start = ((), (), s32[]{:S(2)}) async-start(), calls=%async_computation.14 | async-start | bytes 5242880 | tf_op jit(solution)/shard_map/all_gather | solution.py:161
  154.4 261.6 %all-gather.18.cloned.1.call-start = ((), (), s32[]{:S(2)}) async-start(), calls=%async_computation.15 | async-start | bytes 9437184 | tf_op jit(solution)/shard_map/all_gather | solution.py:146
  155.0 318.8 %all-gather.20.cloned.1.call-start = ((), (), s32[]{:S(2)}) async-start(), calls=%async_computation.16 | async-start | bytes 9437184 | tf_op jit(solution)/shard_map/all_gather | solution.py:148
  155.7 400.8 %reduce-scatter.24.cloned.1.call-start = ((), (), s32[]{:S(2)}) async-start(), calls=%async_computation.20 | async-start | bytes 5242880 | tf_op jit(solution)/shard_map/reduce_scatter | solution.py:239
  318.3 3.2 copy-start.19
  328.7 3.8 copy-start.25
  338.9 3.8 copy-start.25
  347.8 3.6 copy-start.5
  347.8 3.6 copy-start.22
  363.0 3.6 copy-start.5
  363.0 3.6 copy-start.22
  375.9 5.0 copy-start.7
  387.5 6.9 copy-start.11
  389.7 16.2 %copy-start.14 = (bf16[1024,1,512]{2,0,1:T(8,128)(2,1)}, bf16[1024,1,512]{2,0,1:T(8,128)(2,1)S(1)}, u32[]{:S(2)}) copy-start(bf16[1024,1,512]{2,0,1:T(8,128)(2,1)S(1)} %copy.145) | copy-start | bytes 3145732
  394.4 11.4 copy-start.16
  405.9 67.9 %copy-start.35 = (f32[1,2048]{1,0:T(1,128)S(1)}, f32[1,2048]{1,0:T(1,128)}, u32[]{:S(2)}) copy-start(f32[1,2048]{1,0:T(1,128)} %add.225) | copy-start | bytes 24580
  405.9 226.6 %reduce-scatter.22.cloned.1.call-start = ((), (), s32[]{:S(2)}) async-start(), calls=%async_computation.19 | async-start | bytes 5242880 | tf_op jit(solution)/shard_map/reduce_scatter | solution.py:242
  473.8 35.0 %copy-start.44 = (bf16[2048,2048]{1,0:T(8,128)(2,1)S(1)}, bf16[2048,2048]{1,0:T(8,128)(2,1)}, u32[]{:S(2)}) copy-start(bf16[2048,2048]{1,0:T(8,128)(2,1)} %all-gather.18.cloned.1.call-done) | copy-start | bytes 25165828
  519.7 260.2 %reduce-scatter.20.cloned.1.call-start = ((), (), s32[]{:S(2)}) async-start(), calls=%async_computation.17 | async-start | bytes 10485760 | tf_op jit(solution)/shard_map/reduce_scatter | solution.py:184
  532.2 12.7 copy-start.21
  550.6 81.9 %copy-start.2 = (bf16[256,2048]{1,0:T(8,128)(2,1)S(1)}, bf16[256,2048]{1,0:T(8,128)(2,1)}, u32[]{:S(2)}) copy-start(bf16[256,2048]{1,0:T(8,128)(2,1)} %param.15) | copy-start | bytes 3145732
  550.6 81.9 %copy-start.30 = (f32[1,2048]{1,0:T(1,128)S(1)}, f32[1,2048]{1,0:T(1,128)}, u32[]{:S(2)}) copy-start(f32[1,2048]{1,0:T(1,128)} %copy-done.29) | copy-start | bytes 24580
  550.6 81.9 %copy-start.32 = (f32[1,2048]{1,0:T(1,128)S(1)}, f32[1,2048]{1,0:T(1,128)}, u32[]{:S(2)}) copy-start(f32[1,2048]{1,0:T(1,128)} %copy-done.31) | copy-start | bytes 24580
  550.6 81.9 %copy-start.34 = (f32[256]{0:T(256)S(1)}, f32[256]{0:T(256)}, u32[]{:S(2)}) copy-start(f32[256]{0:T(256)} %copy-done.33) | copy-start | bytes 3076
  550.7 84.6 %copy-start.41 = (f32[256]{0:T(256)S(1)}, f32[256]{0:T(256)}, u32[]{:S(2)}) copy-start(f32[256]{0:T(256)} %copy-done.40) | copy-start | bytes 3076
  550.7 84.6 %copy-start.39 = (f32[256]{0:T(256)S(1)}, f32[256]{0:T(256)}, u32[]{:S(2)}) copy-start(f32[256]{0:T(256)} %copy-done.38) | copy-start | bytes 3076
  550.7 287.1 %reduce-scatter.34.cloned.1.call-start = ((), (), s32[]{:S(2)}) async-start(), calls=%async_computation.25 | async-start | bytes 147456
  555.0 301.0 %reduce-scatter.36.cloned.1.call-start = ((), (), s32[]{:S(2)}) async-start(), calls=%async_computation.26 | async-start | bytes 1179648
  556.5 223.4 %copy-start.36 = (f32[1,2048]{1,0:T(1,128)S(1)}, f32[1,2048]{1,0:T(1,128)}, u32[]{:S(2)}) copy-start(f32[1,2048]{1,0:T(1,128)} %get-tuple-element.328) | copy-start | bytes 24580
  556.5 223.4 %copy-start.37 = (f32[1,2048]{1,0:T(1,128)S(1)}, f32[1,2048]{1,0:T(1,128)}, u32[]{:S(2)}) copy-start(f32[1,2048]{1,0:T(1,128)} %get-tuple-element.329) | copy-start | bytes 24580
  556.5 439.3 %reduce-scatter.38.cloned.1.call-start = ((), (), s32[]{:S(2)}) async-start(), calls=%async_computation.27 | async-start | bytes 1081344
  556.6 223.3 %copy-start.4 = (bf16[256,2048]{1,0:T(8,128)(2,1)S(1)}, bf16[256,2048]{1,0:T(8,128)(2,1)}, u32[]{:S(2)}) copy-start(bf16[256,2048]{1,0:T(8,128)(2,1)} %reduce-scatter.24.cloned.1.call-done) | copy-start | bytes 3145732
  640.1 491.4 %reduce-scatter.40.cloned.1.call-start = ((), (), s32[]{:S(2)}) async-start(), calls=%async_computation.28 | async-start | bytes 1081344
  786.3 396.4 %reduce-scatter.28.cloned.1.call-start = ((), (), s32[]{:S(2)}) async-start(), calls=%async_computation.22 | async-start | bytes 4718592 | tf_op jit(solution)/shard_map/reduce_scatter | solution.py:258
  793.2 485.6 %reduce-scatter.26.cloned.1.call-start = ((), (), s32[]{:S(2)}) async-start(), calls=%async_computation.21 | async-start | bytes 14155776 | tf_op jit(solution)/shard_map/reduce_scatter | solution.py:256
  806.7 592.1 %reduce-scatter.32.cloned.1.call-start = ((), (), s32[]{:S(2)}) async-start(), calls=%async_computation.24 | async-start | bytes 18874368 | tf_op jit(solution)/shard_map/reduce_scatter | solution.py:261
  822.1 696.9 %reduce-scatter.30.cloned.1.call-start = ((), (), s32[]{:S(2)}) async-start(), calls=%async_computation.23 | async-start | bytes 18874368 | tf_op jit(solution)/shard_map/reduce_scatter | solution.py:259
  (25 other events, 42.9 us)
Sparse Core Ops, SparseCore 0:
  9.9 30.8 all-gather.13
  42.3 81.0 all-gather.21
  152.7 78.5 all-gather.9
  233.6 45.0 all-gather.11
  280.7 80.7 all-gather.15
  363.2 52.7 all-gather.17
  417.9 55.8 all-gather.19
  476.0 76.7 reduce-scatter.23
  555.2 77.2 reduce-scatter.21
  634.7 145.1 reduce-scatter.19
  782.9 34.1 reduce-scatter.33
  820.1 35.9 reduce-scatter.35
  858.3 137.3 reduce-scatter.37
  997.9 133.5 reduce-scatter.39
  1135.3 47.4 reduce-scatter.27
  1186.7 92.0 reduce-scatter.25
  1282.8 115.9 reduce-scatter.31
  1402.8 116.1 reduce-scatter.29
where the time goes:
time: 1530 us
  waiting for transfers between devices  1040 us (68%)
  matrix products  177 us (12%)
  blocking collectives  155 us (10%)
  local copies, waits for them, and re-layouts  69 us (5%)
  other arithmetic  58 us (4%)
    unnamed x22, waiting for transfers between devices  293 us
    reduce_scatter x1, waiting for transfers between devices, shards(): lax.psum_scatter(attn_part + jnp.dot(activated, back_weight, preferred_el...  140 us
    reduce_scatter x1, waiting for transfers between devices, shards(): lax.psum_scatter(up_term, 'dp', scatter_dimension=0, tiled=True)  120 us
    reduce_scatter x1, waiting for transfers between devices, shards(): lax.psum_scatter(down_term, 'dp', scatter_dimension=1, tiled=True)  120 us
    reduce_scatter x1, waiting for transfers between devices, shards(): lax.psum_scatter(joined_term, 'dp', scatter_dimension=0, tiled=True)  96 us
    reduce_scatter x1, waiting for transfers between devices, shards(): lax.psum_scatter(grad_second.astype(jnp.bfloat16), 'tensor', scatter_dime...  75.9 us
    all_gather x1, blocking collectives, shards(): lax.all_gather(norm_gains, ('dp', 'tensor'), axis=1, tiled=True)  71.2 us
    all_gather x1, blocking collectives, shards(): lax.all_gather(biases, ('dp', 'tensor'), axis=1, tiled=True)  66 us
  transfers between devices with their start and end apart: 18, of which 13 were waited for; matrix products, arithmetic and copies ran while one was open for 19% of the time, Pallas kernels for 0%

commit v1 on v0

--- a/solution.py
+++ b/solution.py
@@ -1,3 +1,4 @@
+import functools
 import jax
 import jax.numpy as jnp
 from jax import lax
@@ -6,6 +7,36 @@
 ROT = 64
 EPSILON = 1e-05
 ROTARY_BASE = 10000.0
+
+
+def view_body_all(chunk, dev_axis, ndim_at):
+    side_arr, met_up, b_now = (
+        jax.lax.axis_size(dev_axis),
+        jax.lax.axis_index(dev_axis),
+        chunk.shape[ndim_at],
+    )
+    windows = [(dev_j, (dev_j + 1) % side_arr) for dev_j in range(side_arr)]
+    new = jnp.zeros(
+        (*chunk.shape[:ndim_at], side_arr * b_now, *chunk.shape[ndim_at + 1 :]), chunk.dtype
+    )
+    new = lax.dynamic_update_slice_in_dim(new, chunk, met_up * b_now, axis=ndim_at)
+    f_next = val = chunk
+    chunks = [(dev_j, (dev_j - 1) % side_arr) for dev_j in range(side_arr)]
+    wide_out = side_arr // 2
+    for pp in range(1, wide_out + 1):
+        f_next = jax.lax.ppermute(f_next, axis_name=dev_axis, perm=windows)
+        new = lax.dynamic_update_slice_in_dim(
+            new, f_next, (met_up - pp) % side_arr * b_now, axis=ndim_at
+        )
+        if pp < side_arr - wide_out:
+            val = jax.lax.ppermute(val, dev_axis, perm=chunks)
+            new = lax.dynamic_update_slice_in_dim(
+                new, val, (met_up + pp) % side_arr * b_now, axis=ndim_at
+            )
+    return new
+
+
+shape_outputs_on = functools.partial(view_body_all, dev_axis="dp", ndim_at=0)
 
 
 def layer_norm(values, gain_row, shift_row):
@@ -140,7 +171,7 @@
     block_rows = min(512, row_count)
     dp_index = lax.axis_index("dp")
     gathered = (
-        lax.all_gather(proj_weight, "dp", axis=0, tiled=True),
+        shape_outputs_on(proj_weight),
         lax.all_gather(proj_bias, "dp", axis=2, tiled=True),
         lax.all_gather(out_weight, "dp", axis=1, tiled=True),
         lax.all_gather(up_weight, "dp", axis=0, tiled=True),

time: 1530 us -> 1640 us (1.072)
  waiting for transfers between devices: 1040 us -> 1120 us
    all_gather x1, waiting for transfers between devices: 0.01 us -> 73.4 us  [shards(): grad_rows = lax.all_gather(cotangent, 'tensor', axis=0, tiled=True)]
    all_gather x1, waiting for transfers between devices: 47.5 us -> 0.01 us  [shards(): lax.all_gather(first_local.astype(jnp.bfloat16), 'tensor', axis=0, tiled=...]
    all_gather x1, waiting for transfers between devices: 47.4 us -> 0.02 us  [shards(): lax.all_gather(proj_weight, 'dp', axis=0, tiled=True)]
    all_gather x1, waiting for transfers between devices: 10 us -> 54.5 us  [shards(): lax.all_gather(up_weight, 'dp', axis=0, tiled=True)]
    all_gather x1, waiting for transfers between devices: 0.02 us -> 32.5 us  [shards(): lax.all_gather(second_local.astype(jnp.bfloat16), 'tensor', axis=0, tiled...]
    ppermute x0 -> x7, waiting for transfers between devices: none -> 17.4 us  [the longest x4 17 us: view_body_all(): f_next = jax.lax.ppermute(f_next, axis_name=dev_axis, perm=windows)]
    unnamed x94 -> x96, local copies, waits for them, and re-layouts: 34.8 us -> 25.5 us
  transfers between devices with their start and end apart: 18 -> 25, of which waited for: 13 -> 16; matrix products, arithmetic and copies ran while one was open for 19% -> 18% of each run, Pallas kernels for 0% -> 0%
where the time goes in v1:
time: 1640 us; the launch traced here: 1630 us
  waiting for transfers between devices  1120 us (68%)
  matrix products  190 us (12%)
  blocking collectives  170 us (10%)
  local copies, waits for them, and re-layouts  69.5 us (4%)
  other arithmetic  56.5 us (3%)
    unnamed x22, waiting for transfers between devices  293 us
    reduce_scatter x1, waiting for transfers between devices, shards(): lax.psum_scatter(attn_part + jnp.dot(activated, back_weight, preferred_el...  140 us
    reduce_scatter x1, waiting for transfers between devices, shards(): lax.psum_scatter(up_term, 'dp', scatter_dimension=0, tiled=True)  120 us
    reduce_scatter x1, waiting for transfers between devices, shards(): lax.psum_scatter(down_term, 'dp', scatter_dimension=1, tiled=True)  120 us
    reduce_scatter x1, waiting for transfers between devices, shards(): lax.psum_scatter(joined_term, 'dp', scatter_dimension=0, tiled=True)  96 us
    reduce_scatter x1, waiting for transfers between devices, shards(): lax.psum_scatter(grad_second.astype(jnp.bfloat16), 'tensor', scatter_dime...  75.7 us
    all_gather x1, waiting for transfers between devices, shards(): grad_rows = lax.all_gather(cotangent, 'tensor', axis=0, tiled=True)  73.4 us
    all_gather x1, blocking collectives, shards(): lax.all_gather(norm_gains, ('dp', 'tensor'), axis=1, tiled=True)  70 us
  transfers between devices with their start and end apart: 25, of which 16 were waited for; matrix products, arithmetic and copies ran while one was open for 18% of the time, Pallas kernels for 0%

profile of v1, /device:TPU:0, one launch (start us, length us, event | category | flops | bytes accessed | tf_op | source)
XLA Modules:
  0.0 1631.3 jit_solution(13693049485644384767)
XLA Ops:
  10.4 70.0 %all-gather = bf16[32,64,2]{1,2,0:T(2,128)(2,1)S(1)} all-gather(bf16[1,64,2]{1,2,0:T(2,128)(2,1)} %bitcast.182), channel_id=1, replica_groups=mesh['dp'=8,'tensor'=4] {'dp','tensor'}, dimensions={0}, use_global_device_ids=true | all-gather | bytes 8448 | tf_op jit(solution)/shard_map/all_gather | solution.py:183
  80.5 63.8 %all-gather.1 = bf16[32,64,4]{1,2,0:T(4,128)(2,1)S(1)} all-gather(bf16[1,64,4]{1,2,0:T(4,128)(2,1)} %bitcast.181), channel_id=1, replica_groups=mesh['dp'=8,'tensor'=4] {'dp','tensor'}, dimensions={0}, use_global_device_ids=true | all-gather | bytes 16896 | tf_op jit(solution)/shard_map/all_gather | solution.py:184
  145.0 3.3 fusion.58
  151.8 2.6 collective-permute-start.1
  154.4 12.6 collective-permute-done
  167.3 15.3 all_gather.39
  184.5 21.1 %all_gather.43 = bf16[1,2048]{1,0:T(2,128)(2,1)S(1)} all-gather(bf16[1,256]{1,0:T(2,128)(2,1)S(1)} %copy-done.45), channel_id=1, replica_groups=mesh['dp'=8,'tensor'=4] {'dp'}, dimensions={1}, use_global_device_ids=true | all-gather | bytes 4608 | tf_op jit(solution)/shard_map/all_gather | solution.py:178
  206.2 3.5 broadcast_in_dim.60
  211.9 3.0 broadcast_multiply_fusion
  228.0 4.4 collective-permute-done.6
  234.7 10.2 broadcast_add_fusion
  259.1 2.7 subtract_convert_fusion.2
  261.8 2.8 pad_maximum_fusion.1
  264.7 73.4 %all-gather.20.cloned.1.call-done = bf16[1024,2048]{1,0:T(8,128)(2,1)} async-done(((bf16[256,2048]{1,0:T(8,128)(2,1)}), bf16[1024,2048]{1,0:T(8,128)(2,1)}) %all-gather.20.cloned.1.call-update) | async-done | bytes 4194320 | tf_op jit(solution)/shard_map/all_gather | solution.py:222
  338.1 6.2 convolution_convert_fusion.1
  344.4 19.1 %while.27 = (s32[]{:T(128)}, bf16[2,512,2,256]{3,1,2,0:T(8,128)(2,1)}, f32[2,2,512]{2,1,0:T(2,128)S(1)}, s32[2]{0:T(128)S(1)}, s32[1024]{0:T(1024)S(1)}, /*index...) while((s32[]{:T(128)}, ...), condition=%wide.region_5.6_spmd, body=%wide.region_2.0_spmd.sunk | while | flops 1087897088 | bytes 18397868 | solution.py:109
  363.5 40.1 %while.28 = (s32[]{:T(128)}, f32[1024,2,256]{0,2,1:T(8,128)}, f32[1024,2,256]{0,2,1:T(8,128)}, f32[2,512,2,256]{3,1,0,2:T(8,128)}, s32[2]{0:T(128)S(1)}, /*index...) while((s32[]{:T(128)}, f32[1024,2,256]{0,2,1:T(8,128)}, ...), condition=%wide.region_12.13_spmd.clone, body=%wide.region_10.12_spmd.clone.sunk | while | flops 2704539136 | bytes 123775488 | solution.py:150
  372.4 3.4 bitcast_add_fusion.4
  379.0 3.0 bitcast_add_fusion.5
  391.0 4.3 bitcast_add_fusion.4
  398.8 4.8 bitcast_add_fusion.5
  417.8 3.1 convert.66
  422.5 11.5 bitcast_convert_fusion
  434.0 32.5 %all-gather.14.cloned.1.call-done = bf16[1024,2048]{1,0:T(8,128)(2,1)} async-done(((bf16[256,2048]{1,0:T(8,128)(2,1)}), bf16[1024,2048]{1,0:T(8,128)(2,1)}) %all-gather.14.cloned.1.call-update) | async-done | bytes 4194320 | tf_op jit(solution)/shard_map/all_gather | solution.py:192
  466.6 54.5 %all-gather.16.cloned.1.call-done = bf16[2048,2048]{1,0:T(8,128)(2,1)} async-done(((bf16[256,2048]{1,0:T(8,128)(2,1)}), bf16[2048,2048]{1,0:T(8,128)(2,1)}) %all-gather.16.cloned.1.call-update) | async-done | bytes 8388624 | tf_op jit(solution)/shard_map/all_gather | solution.py:177
  521.1 14.7 fusion.78
  535.8 43.1 %all-gather.18.cloned.1.call-done = bf16[2048,2048]{1,0:T(8,128)(2,1)} async-done(((bf16[2048,256]{1,0:T(8,128)(2,1)}), bf16[2048,2048]{1,0:T(8,128)(2,1)}) %all-gather.18.cloned.1.call-update) | async-done | bytes 8388624 | tf_op jit(solution)/shard_map/all_gather | solution.py:179
  578.9 33.1 %convert_reduce_fusion = (f32[2048]{0:T(1024)S(1)}, bf16[1024,2048]{1,0:T(8,128)(2,1)S(1)}, f32[1024,2048]{1,0:T(8,128)}) fusion(f32[1024,2048]{1,0:T(8,128)} %fusion.78, f32[2048]{0:T(1024)S(1)} %bitcast.166, bf16[1024,2048]{1,0:T(8,128)(2,1)} %all-gather.20.cloned.1.call-done, bf16[2048,2048]{1,0:T(8,128)(2,1)} %all-gather.18.cloned.1.call-done), kind=kOutput, calls=%fused_computation.50 | convolution fusion | flops 8747218944 | bytes 33570816 | tf_op jit(solution)/shard_map/nd,fd->nf/dot_general | solution.py:232
  613.9 10.9 convolution_convert_fusion
  627.4 10.0 multiply_convert_fusion.1
  637.4 12.7 fusion.79
  650.2 5.6 convolution_add_fusion
  661.9 75.7 %reduce-scatter.22.cloned.1.call-done = bf16[256,2048]{1,0:T(8,128)(2,1)} async-done(((bf16[1024,2048]{1,0:T(8,128)(2,1)}), bf16[256,2048]{1,0:T(8,128)(2,1)}) %reduce-scatter.22.cloned.1.call-update) | async-done | bytes 1048592 | tf_op jit(solution)/shard_map/reduce_scatter | solution.py:273
  737.6 2.7 fusion.62
  740.4 3.3 fusion.67
  745.2 139.7 %reduce-scatter.20.cloned.1.call-done = f32[256,2048]{1,0:T(8,128)} async-done(((f32[1024,2048]{1,0:T(8,128)}), f32[256,2048]{1,0:T(8,128)}) %reduce-scatter.20.cloned.1.call-update) | async-done | bytes 2097168 | tf_op jit(solution)/shard_map/reduce_scatter | solution.py:215
  884.9 5.0 convert_reduce_fusion.5
  891.6 6.5 fusion.80
  900.1 11.7 fusion.41
  911.8 15.2 fusion.82
  927.4 15.2 fusion.81
  944.1 17.1 %reduce-scatter.36.cloned.1.call-done = f32[256,1]{1,0:T(8,128)} async-done(((f32[2048,1]{1,0:T(8,128)}), f32[256,1]{1,0:T(8,128)}) %reduce-scatter.36.cloned.1.call-update) | async-done | bytes 1040
  962.7 138.1 %reduce-scatter.38.cloned.1.call-done = f32[64,2]{1,0:T(8,128)} async-done(((f32[2048,2]{1,0:T(8,128)}), f32[64,2]{1,0:T(8,128)}) %reduce-scatter.38.cloned.1.call-update) | async-done | bytes 528
  1102.3 134.6 %reduce-scatter.40.cloned.1.call-done = f32[64,4]{1,0:T(8,128)} async-done(((f32[2048,4]{1,0:T(8,128)}), f32[64,4]{1,0:T(8,128)}) %reduce-scatter.40.cloned.1.call-update) | async-done | bytes 1040
  1238.3 49.7 %reduce-scatter.28.cloned.1.call-done = f32[512,256]{1,0:T(8,128)} async-done(((f32[512,2048]{1,0:T(8,128)}), f32[512,256]{1,0:T(8,128)}) %reduce-scatter.28.cloned.1.call-update) | async-done | bytes 524304 | tf_op jit(solution)/shard_map/reduce_scatter | solution.py:289
  1288.0 96.0 %reduce-scatter.26.cloned.1.call-done = f32[256,3,512]{2,0,1:T(8,128)} async-done(((f32[2048,3,512]{2,0,1:T(8,128)}), f32[256,3,512]{2,0,1:T(8,128)}) %reduce-scatter.26.cloned.1.call-update) | async-done | bytes 1572880 | tf_op jit(solution)/shard_map/reduce_scatter | solution.py:287
  1384.0 120.0 %reduce-scatter.32.cloned.1.call-done = f32[2048,256]{1,0:T(8,128)} async-done(((f32[2048,2048]{1,0:T(8,128)}), f32[2048,256]{1,0:T(8,128)}) %reduce-scatter.32.cloned.1.call-update) | async-done | bytes 2097168 | tf_op jit(solution)/shard_map/reduce_scatter | solution.py:292
  1504.0 120.2 %reduce-scatter.30.cloned.1.call-done = f32[256,2048]{1,0:T(8,128)} async-done(((f32[2048,2048]{1,0:T(8,128)}), f32[256,2048]{1,0:T(8,128)}) %reduce-scatter.30.cloned.1.call-update) | async-done | bytes 2097168 | tf_op jit(solution)/shard_map/reduce_scatter | solution.py:290
  (287 shorter events, 115.2 us)
Async XLA Ops:
  7.2 227.6 %all-gather.10.cloned.1.call-start = ((), (), s32[]{:S(2)}) async-start(), calls=%async_computation.11 | async-start | bytes 5242880 | tf_op jit(solution)/shard_map/all_gather | solution.py:191
  8.7 142.4 %copy-start.35 = (f32[256]{0:T(256)}, f32[256]{0:T(256)S(1)}, u32[]{:S(2)}) copy-start(f32[256]{0:T(256)S(1)} %broadcast_multiply_fusion.1) | copy-start | bytes 3076
  10.3 70.0 %copy-start.42 = (f32[256]{0:T(256)}, f32[256]{0:T(256)S(1)}, u32[]{:S(2)}) copy-start(f32[256]{0:T(256)S(1)} %fusion.61) | copy-start | bytes 3076
  10.4 141.3 %copy-start.40 = (f32[256]{0:T(256)}, f32[256]{0:T(256)S(1)}, u32[]{:S(2)}) copy-start(f32[256]{0:T(256)S(1)} %fusion.71) | copy-start | bytes 3076
  80.4 71.2 %copy-start.31 = (f32[1,2048]{1,0:T(1,128)}, f32[1,2048]{1,0:T(1,128)S(1)}, u32[]{:S(2)}) copy-start(f32[1,2048]{1,0:T(1,128)S(1)} %get-tuple-element.332) | copy-start | bytes 24580
  80.5 71.2 %copy-start.33 = (f32[1,2048]{1,0:T(1,128)}, f32[1,2048]{1,0:T(1,128)S(1)}, u32[]{:S(2)}) copy-start(f32[1,2048]{1,0:T(1,128)S(1)} %get-tuple-element.333) | copy-start | bytes 24580
  145.0 22.1 %copy-start.44 = (bf16[3,2,32]{2,1,0:T(2,128)(2,1)S(1)}, bf16[3,2,32]{2,1,0:T(2,128)(2,1)}, u32[]{:S(2)}) copy-start(bf16[3,2,32]{2,1,0:T(2,128)(2,1)} %param.18) | copy-start | bytes 1156
  148.4 36.1 %copy-start.45 = (bf16[1,256]{1,0:T(2,128)(2,1)S(1)}, bf16[1,256]{1,0:T(2,128)(2,1)}, u32[]{:S(2)}) copy-start(bf16[1,256]{1,0:T(2,128)(2,1)} %param.21) | copy-start | bytes 1540
  148.4 116.3 %all-gather.12.cloned.1.call-start = ((), (), s32[]{:S(2)}) async-start(), calls=%async_computation.12 | async-start | bytes 2359296 | tf_op jit(solution)/shard_map/all_gather | solution.py:176
  149.2 189.0 %all-gather.20.cloned.1.call-start = ((), (), s32[]{:S(2)}) async-start(), calls=%async_computation.17 | async-start | bytes 5242880 | tf_op jit(solution)/shard_map/all_gather | solution.py:222
  149.9 272.6 %all-gather.22.cloned.1.call-start = ((), (), s32[]{:S(2)}) async-start(), calls=%async_computation.19 | async-start | bytes 7077888 | tf_op jit(solution)/shard_map/all_gather | solution.py:224
  150.5 316.1 %all-gather.14.cloned.1.call-start = ((), (), s32[]{:S(2)}) async-start(), calls=%async_computation.13 | async-start | bytes 5242880 | tf_op jit(solution)/shard_map/all_gather | solution.py:192
  151.1 370.0 %all-gather.16.cloned.1.call-start = ((), (), s32[]{:S(2)}) async-start(), calls=%async_computation.14 | async-start | bytes 9437184 | tf_op jit(solution)/shard_map/all_gather | solution.py:177
  151.7 427.2 %all-gather.18.cloned.1.call-start = ((), (), s32[]{:S(2)}) async-start(), calls=%async_computation.15 | async-start | bytes 9437184 | tf_op jit(solution)/shard_map/all_gather | solution.py:179
  151.7 15.3 collective-permute-start
  151.8 30.9 %collective-permute-start.1 = (bf16[256,3,512]{2,0,1:T(8,128)(2,1)S(1)}, bf16[256,3,512]{2,0,1:T(8,128)(2,1)S(1)}, u32[]{:S(2)}, u32[]{:S(2)}) collective-permute-start(bf16[256,3,512]{2,0,1:T(8,128)(2,1)S(1)} %copy-done.24), channel_id=1, source_target_pairs={{0,28},{4,0},{8,4},{12,8},{16,12},{20,16},{24,20},{28,24},{1,29},{... | collective-permute-start | bytes 2359304 | tf_op jit(solution)/shard_map/ppermute | solution.py:32
  167.1 17.0 %copy-start.28 = (bf16[256,3,512]{2,0,1:T(8,128)(2,1)}, bf16[256,3,512]{2,0,1:T(8,128)(2,1)S(1)}, u32[]{:S(2)}) copy-start(bf16[256,3,512]{2,0,1:T(8,128)(2,1)S(1)} %collective-permute-done) | copy-start | bytes 2359300
  167.1 16.9 %collective-permute-start.2 = (bf16[256,3,512]{2,0,1:T(8,128)(2,1)S(1)}, bf16[256,3,512]{2,0,1:T(8,128)(2,1)S(1)}, u32[]{:S(2)}, u32[]{:S(2)}) collective-permute-start(bf16[256,3,512]{2,0,1:T(8,128)(2,1)S(1)} %collective-permute-done), channel_id=1, source_target_pairs={{0,4},{4,8},{8,12},{12,16},{16,20},{20,24},{24,28},{28,0},{1,5},{5... | collective-permute-start | bytes 2359304 | tf_op jit(solution)/shard_map/ppermute | solution.py:27
  167.1 494.8 %reduce-scatter.24.cloned.1.call-start = ((), (), s32[]{:S(2)}) async-start(), calls=%async_computation.20 | async-start | bytes 5242880 | tf_op jit(solution)/shard_map/reduce_scatter | solution.py:270
  182.6 28.0 %copy-start.30 = (bf16[256,3,512]{2,0,1:T(8,128)(2,1)}, bf16[256,3,512]{2,0,1:T(8,128)(2,1)S(1)}, u32[]{:S(2)}) copy-start(bf16[256,3,512]{2,0,1:T(8,128)(2,1)S(1)} %collective-permute-done.1) | copy-start | bytes 2359300
  182.6 28.0 %collective-permute-start.3 = (bf16[256,3,512]{2,0,1:T(8,128)(2,1)S(1)}, bf16[256,3,512]{2,0,1:T(8,128)(2,1)}, u32[]{:S(2)}, u32[]{:S(2)}) collective-permute-start(bf16[256,3,512]{2,0,1:T(8,128)(2,1)S(1)} %collective-permute-done.1), channel_id=1, source_target_pairs={{0,28},{4,0},{8,4},{12,8},{16,12},{20,16},{24,20},{28,24},{1,29},{... | collective-permute-start | bytes 2359304 | tf_op jit(solution)/shard_map/ppermute | solution.py:32
  184.0 32.6 %collective-permute-start.4 = (bf16[256,3,512]{2,0,1:T(8,128)(2,1)S(1)}, bf16[256,3,512]{2,0,1:T(8,128)(2,1)}, u32[]{:S(2)}, u32[]{:S(2)}) collective-permute-start(bf16[256,3,512]{2,0,1:T(8,128)(2,1)S(1)} %collective-permute-done.2), channel_id=1, source_target_pairs={{0,4},{4,8},{8,12},{12,16},{16,20},{20,24},{24,28},{28,0},{1,5},{5... | collective-permute-start | bytes 2359304 | tf_op jit(solution)/shard_map/ppermute | solution.py:27
  184.3 26.4 %copy-start.27 = (s32[1024]{0:T(1024)S(1)}, s32[1024]{0:T(1024)}, u32[]{:S(2)}) copy-start(s32[1024]{0:T(1024)} %param.16) | copy-start | bytes 12292
  210.7 13.9 collective-permute-start.5
  216.6 15.8 collective-permute-start.6
  417.8 16.1 copy-start.17
  434.0 144.9 %copy-start.37 = (f32[1,2048]{1,0:T(1,128)S(1)}, f32[1,2048]{1,0:T(1,128)}, u32[]{:S(2)}) copy-start(f32[1,2048]{1,0:T(1,128)} %add.302) | copy-start | bytes 24580
  434.0 303.6 %reduce-scatter.22.cloned.1.call-start = ((), (), s32[]{:S(2)}) async-start(), calls=%async_computation.18 | async-start | bytes 5242880 | tf_op jit(solution)/shard_map/reduce_scatter | solution.py:273
  578.9 35.1 %copy-start.46 = (bf16[2048,2048]{1,0:T(8,128)(2,1)S(1)}, bf16[2048,2048]{1,0:T(8,128)(2,1)}, u32[]{:S(2)}) copy-start(bf16[2048,2048]{1,0:T(8,128)(2,1)} %all-gather.16.cloned.1.call-done) | copy-start | bytes 25165828
  624.8 260.1 %reduce-scatter.20.cloned.1.call-start = ((), (), s32[]{:S(2)}) async-start(), calls=%async_computation.16 | async-start | bytes 10485760 | tf_op jit(solution)/shard_map/reduce_scatter | solution.py:215
  637.4 12.7 copy-start.26
  655.8 81.8 %copy-start.6 = (bf16[256,2048]{1,0:T(8,128)(2,1)S(1)}, bf16[256,2048]{1,0:T(8,128)(2,1)}, u32[]{:S(2)}) copy-start(bf16[256,2048]{1,0:T(8,128)(2,1)} %param.15) | copy-start | bytes 3145732
  655.8 81.8 %copy-start.32 = (f32[1,2048]{1,0:T(1,128)S(1)}, f32[1,2048]{1,0:T(1,128)}, u32[]{:S(2)}) copy-start(f32[1,2048]{1,0:T(1,128)} %copy-done.31) | copy-start | bytes 24580
  655.8 81.7 %copy-start.34 = (f32[1,2048]{1,0:T(1,128)S(1)}, f32[1,2048]{1,0:T(1,128)}, u32[]{:S(2)}) copy-start(f32[1,2048]{1,0:T(1,128)} %copy-done.33) | copy-start | bytes 24580
  655.9 81.7 %copy-start.36 = (f32[256]{0:T(256)S(1)}, f32[256]{0:T(256)}, u32[]{:S(2)}) copy-start(f32[256]{0:T(256)} %copy-done.35) | copy-start | bytes 3076
  655.9 84.5 %copy-start.43 = (f32[256]{0:T(256)S(1)}, f32[256]{0:T(256)}, u32[]{:S(2)}) copy-start(f32[256]{0:T(256)} %copy-done.42) | copy-start | bytes 3076
  655.9 84.5 %copy-start.41 = (f32[256]{0:T(256)S(1)}, f32[256]{0:T(256)}, u32[]{:S(2)}) copy-start(f32[256]{0:T(256)} %copy-done.40) | copy-start | bytes 3076
  655.9 286.7 %reduce-scatter.34.cloned.1.call-start = ((), (), s32[]{:S(2)}) async-start(), calls=%async_computation.25 | async-start | bytes 147456
  660.3 300.9 %reduce-scatter.36.cloned.1.call-start = ((), (), s32[]{:S(2)}) async-start(), calls=%async_computation.26 | async-start | bytes 1179648
  661.7 223.2 %copy-start.38 = (f32[1,2048]{1,0:T(1,128)S(1)}, f32[1,2048]{1,0:T(1,128)}, u32[]{:S(2)}) copy-start(f32[1,2048]{1,0:T(1,128)} %get-tuple-element.328) | copy-start | bytes 24580
  661.8 223.2 %copy-start.39 = (f32[1,2048]{1,0:T(1,128)S(1)}, f32[1,2048]{1,0:T(1,128)}, u32[]{:S(2)}) copy-start(f32[1,2048]{1,0:T(1,128)} %get-tuple-element.329) | copy-start | bytes 24580
  661.8 439.1 %reduce-scatter.38.cloned.1.call-start = ((), (), s32[]{:S(2)}) async-start(), calls=%async_computation.27 | async-start | bytes 1081344
  661.8 223.1 %copy-start.7 = (bf16[256,2048]{1,0:T(8,128)(2,1)S(1)}, bf16[256,2048]{1,0:T(8,128)(2,1)}, u32[]{:S(2)}) copy-start(bf16[256,2048]{1,0:T(8,128)(2,1)} %reduce-scatter.24.cloned.1.call-done) | copy-start | bytes 3145732
  745.2 491.7 %reduce-scatter.40.cloned.1.call-start = ((), (), s32[]{:S(2)}) async-start(), calls=%async_computation.28 | async-start | bytes 1081344
  891.4 396.6 %reduce-scatter.28.cloned.1.call-start = ((), (), s32[]{:S(2)}) async-start(), calls=%async_computation.22 | async-start | bytes 4718592 | tf_op jit(solution)/shard_map/reduce_scatter | solution.py:289
  898.2 485.8 %reduce-scatter.26.cloned.1.call-start = ((), (), s32[]{:S(2)}) async-start(), calls=%async_computation.21 | async-start | bytes 14155776 | tf_op jit(solution)/shard_map/reduce_scatter | solution.py:287
  911.8 592.3 %reduce-scatter.32.cloned.1.call-start = ((), (), s32[]{:S(2)}) async-start(), calls=%async_computation.24 | async-start | bytes 18874368 | tf_op jit(solution)/shard_map/reduce_scatter | solution.py:292
  927.1 697.2 %reduce-scatter.30.cloned.1.call-start = ((), (), s32[]{:S(2)}) async-start(), calls=%async_computation.23 | async-start | bytes 18874368 | tf_op jit(solution)/shard_map/reduce_scatter | solution.py:290
  (35 other events, 163.0 us)
Sparse Core Ops, SparseCore 0:
  148.5 78.6 all-gather.9
  229.1 26.5 all-gather.11
  257.3 80.7 all-gather.19
  339.9 43.8 all-gather.21
  385.8 80.7 all-gather.13
  468.3 52.7 all-gather.15
  523.0 55.8 all-gather.17
  581.1 76.7 reduce-scatter.23
  660.3 77.2 reduce-scatter.21
  739.8 145.1 reduce-scatter.19
  887.9 34.1 reduce-scatter.33
  925.2 35.9 reduce-scatter.35
  963.4 137.3 reduce-scatter.37
  1103.0 133.8 reduce-scatter.39
  1240.7 47.2 reduce-scatter.27
  1291.9 92.0 reduce-scatter.25
  1388.0 115.9 reduce-scatter.31
  1508.0 116.1 reduce-scatter.29
